TPU v7x, 512 devices: a whole 4x8x8 slice. The times are simulated.
512 devices in a mesh: blk: 64 (over y, z_hi, core), req: 8 (over z_lo, x).
Axes of the slice: x: 4, y: 8, z: 8 (z_hi: 4, z_lo: 2; z = z_hi * 2 + z_lo), core: 2. Of those that a mesh axis runs over, the one named last changes fastest.
Arguments:
- tokens: bfloat16 [8192, 1024], P('blk'), may hold values from -6 to 6
- w_qkv: bfloat16 [1024, 3, 1024], P(None, None, 'req'), may hold values from -0.1875 to 0.1875
- w_out: bfloat16 [1024, 1024], P('req'), may hold values from -0.75 to 0.75
- k_pages: bfloat16 [1280, 128, 1024], P('blk', None, 'req'), may hold values from -512 to 512
- v_pages: bfloat16 [1280, 128, 1024], P('blk', None, 'req'), may hold values from -18 to 18
- page_table: int32 [320, 4], P('blk'), may hold values from 0 to 19, as said below
- cache_lens: int32 [320], P('blk'), may hold values from 1 to 512, as said below
- norm1_gain: float32 [1024], replicated, may hold values from 0.5 to 1.5
- norm1_shift: float32 [1024], replicated, may hold values from -3 to 3
- w_up: bfloat16 [1024, 4096], P(None, 'blk'), may hold values from -0.1875 to 0.1875
- w_down: bfloat16 [4096, 1024], P('blk'), may hold values from -0.1875 to 0.1875
- norm2_gain: float32 [1024], replicated, may hold values from 0.5 to 1.5
- norm2_shift: float32 [1024], replicated, may hold values from -3 to 3
Outputs:
- layer_out: bfloat16 [8192, 1024], P(('blk', 'req'))
Inputs may be any that keep to these rules, and one draw needn't show every extreme that they name: `page_table`: the 5 rows of one request group name every page of that group's pool exactly once. `cache_lens`: every request group has at least one request whose cache is full.
All inputs are finite; a program needn't handle non-finite values.
Results may differ from a plain program's by a relative error of at most 0.02.
Values may be sent and summed in bfloat16 or wider, within the bound.
A program may use at most 64 MiB of HBM per device.

v0:
```python
import jax
import jax.numpy as jnp
from jax import lax
from jax.sharding import PartitionSpec as P

HD = 64
epsilon = 1e-05
masked_score = -1e30


def layer_norm(values, gain_vec, shift_vec):
    center = values - jnp.mean(values, axis=-1, keepdims=True)
    spread = jnp.mean(center * center, axis=-1, keepdims=True)
    return center * lax.rsqrt(spread + epsilon) * gain_vec + shift_vec


def attend(queries, key_new, value_new, key_pool, value_pool, page_map, lengths):
    requests = page_map.shape[0]
    stretch_len = queries.shape[0] - (requests - 1)
    head_count = key_pool.shape[2]
    head_size = key_pool.shape[3]
    key_seq = key_pool[page_map].reshape(requests, -1, head_count, head_size)
    value_seq = value_pool[page_map].reshape(requests, -1, head_count, head_size)
    scale_factor = head_size ** (-0.5)
    key_span = key_seq.shape[1]
    positions = jnp.arange(key_span)
    prompt_query = queries[:stretch_len]
    cache_scores = (
        jnp.einsum("chd,shd->hcs", prompt_query, key_seq[0], preferred_element_type=jnp.float32)
        * scale_factor
    )
    cache_scores = jnp.where(positions[None, None, :] < lengths[0], cache_scores, masked_score)
    stretch_scores = (
        jnp.einsum(
            "chd,jhd->hcj", prompt_query, key_new[:stretch_len], preferred_element_type=jnp.float32
        )
        * scale_factor
    )
    causal = jnp.arange(stretch_len)[:, None] >= jnp.arange(stretch_len)[None, :]
    stretch_scores = jnp.where(causal[None], stretch_scores, masked_score)
    top_score = jnp.maximum(
        jnp.max(cache_scores, -1, keepdims=True), jnp.max(stretch_scores, -1, keepdims=True)
    )
    cache_exp = jnp.exp(cache_scores - top_score)
    stretch_exp = jnp.exp(stretch_scores - top_score)
    exp_total = jnp.sum(cache_exp, -1, keepdims=True) + jnp.sum(stretch_exp, -1, keepdims=True)
    cache_weight = (cache_exp / exp_total).astype(jnp.bfloat16)
    stretch_weight = (stretch_exp / exp_total).astype(jnp.bfloat16)
    prompt_out = jnp.einsum(
        "hcs,shd->chd", cache_weight, value_seq[0], preferred_element_type=jnp.float32
    )
    prompt_out = prompt_out + jnp.einsum(
        "hcj,jhd->chd", stretch_weight, value_new[:stretch_len], preferred_element_type=jnp.float32
    )
    step_query = queries[stretch_len:]
    step_scores = (
        jnp.einsum("rhd,rshd->rhs", step_query, key_seq[1:], preferred_element_type=jnp.float32)
        * scale_factor
    )
    step_scores = jnp.where(
        positions[None, None, :] < lengths[1:, None, None], step_scores, masked_score
    )
    self_score = (
        jnp.einsum(
            "rhd,rhd->rh", step_query, key_new[stretch_len:], preferred_element_type=jnp.float32
        )[..., None]
        * scale_factor
    )
    step_top = jnp.maximum(jnp.max(step_scores, -1, keepdims=True), self_score)
    step_exp = jnp.exp(step_scores - step_top)
    self_exp = jnp.exp(self_score - step_top)
    step_total = jnp.sum(step_exp, -1, keepdims=True) + self_exp
    step_weight = (step_exp / step_total).astype(jnp.bfloat16)
    self_weight = (self_exp / step_total).astype(jnp.bfloat16)
    step_out = jnp.einsum(
        "rhs,rshd->rhd", step_weight, value_seq[1:], preferred_element_type=jnp.float32
    )
    step_out = step_out + self_weight.astype(jnp.float32) * value_new[stretch_len:].astype(
        jnp.float32
    )
    merged = jnp.concatenate([prompt_out, step_out], axis=0)
    return merged.astype(jnp.bfloat16).reshape(queries.shape[0], head_count * head_size)


def on_device(
    tokens,
    w_qkv,
    w_out,
    k_pages,
    v_pages,
    page_table,
    cache_lens,
    norm1_gain,
    norm1_shift,
    w_up,
    w_down,
    norm2_gain,
    norm2_shift,
):
    tok_rows, model_width = tokens.shape
    head_cols = w_qkv.shape[2]
    head_count = head_cols // HD
    projected = jnp.dot(
        tokens, w_qkv.reshape(model_width, 3 * head_cols), preferred_element_type=jnp.float32
    ).astype(jnp.bfloat16)
    projected = projected.reshape(tok_rows, 3, head_count, HD)
    pool_pages = k_pages.shape[0]
    key_pool = k_pages.reshape(pool_pages, k_pages.shape[1], head_count, HD)
    value_pool = v_pages.reshape(pool_pages, v_pages.shape[1], head_count, HD)
    attended = attend(
        projected[:, 0],
        projected[:, 1],
        projected[:, 2],
        key_pool,
        value_pool,
        page_table,
        cache_lens,
    )
    partial_out = jnp.dot(attended, w_out, preferred_element_type=jnp.float32)
    own_rows = tok_rows // lax.axis_size("req")
    row_first = lax.axis_index("req") * own_rows
    summed = lax.psum(partial_out.astype(jnp.bfloat16), "req").astype(jnp.float32)
    head_mixed = lax.dynamic_slice_in_dim(summed, row_first, own_rows, 0)
    residual = lax.dynamic_slice_in_dim(tokens, row_first, own_rows, 0).astype(jnp.float32)
    normed = layer_norm(residual + head_mixed, norm1_gain, norm1_shift).astype(jnp.bfloat16)
    hidden = jax.nn.gelu(
        jnp.dot(
            lax.all_gather(normed, "blk", axis=0, tiled=True),
            w_up,
            preferred_element_type=jnp.float32,
        ),
        approximate=False,
    ).astype(jnp.bfloat16)
    branch = lax.psum_scatter(
        jnp.dot(hidden, w_down, preferred_element_type=jnp.float32),
        "blk",
        scatter_dimension=0,
        tiled=True,
    )
    return layer_norm(normed.astype(jnp.float32) + branch, norm2_gain, norm2_shift).astype(
        jnp.bfloat16
    )


def solution(mesh):
    return jax.shard_map(
        on_device,
        mesh=mesh,
        in_specs=(
            P("blk", None),
            P(None, None, "req"),
            P("req", None),
            P("blk", None, "req"),
            P("blk", None, "req"),
            P("blk", None),
            P("blk"),
            P(),
            P(),
            P(None, "blk"),
            P("blk", None),
            P(),
            P(),
        ),
        out_specs=P(("blk", "req"), None),
        check_vma=False,
    )
```

profile of v0, /device:TPU:2, one launch (start us, length us, event | category | flops | bytes accessed | tf_op | source)
XLA Modules:
  0.0 365.7 jit_solution(5662125291629240805)
XLA Ops:
  6.6 1.5 copy.45
  8.1 1.3 convolution_convert_fusion.1
  9.4 0.1 copy.46
  10.1 0.3 copy.47
  10.5 0.7 gather_fusion.1
  11.2 0.3 copy.50
  11.6 0.2 slice.82
  11.8 0.5 copy-done.3
  12.2 0.3 copy.42
  12.6 0.7 gather_fusion
  13.3 0.3 copy.51
  13.7 0.2 slice.86
  13.9 0.3 fusion.105
  14.3 0.2 fusion.5
  14.7 0.2 fusion.69
  14.9 0.2 fusion.3
  15.2 0.1 copy.61
  15.3 0.2 fusion.106
  15.6 0.2 fusion.7
  15.9 0.3 fusion.18
  16.2 0.2 fusion.2
  16.5 1.0 convolution_convert_fusion
  17.6 88.0 %all-reduce.2.cloned.1.call-done = bf16[128,1024]{1,0:T(8,128)(2,1)} async-done(((bf16[128,1024]{1,0:T(8,128)(2,1)}), bf16[128,1024]{1,0:T(8,128)(2,1)}) %all-reduce.2.cloned.1.call-update) | async-done | bytes 262160 | tf_op jit(solution)/shard_map/psum | solution.py:122
  105.6 0.9 fusion.62
  106.5 1.0 multiply_reduce_fusion.1
  107.5 1.5 add_convert_fusion.1
  109.0 86.5 %all-gather.2.cloned.1.call-done = bf16[1024,1024]{1,0:T(8,128)(2,1)} async-done(((bf16[16,1024]{1,0:T(8,128)(2,1)}), bf16[1024,1024]{1,0:T(8,128)(2,1)}) %all-gather.2.cloned.1.call-update) | async-done | bytes 2097168 | tf_op jit(solution)/shard_map/all_gather | solution.py:128
  195.5 5.3 %fusion.19 = f32[1024,1024]{1,0:T(8,128)} fusion(bf16[64,1024]{1,0:T(8,128)(2,1)S(1)} %copy-done.9, bf16[1024,1024]{1,0:T(8,128)(2,1)} %all-gather.2.cloned.1.call-done, bf16[1024,64]{0,1:T(8,128)(2,1)S(1)} %copy-done.10), kind=kOutput, calls=%fused_computation.37 | convolution fusion | flops 272695296 | bytes 6553600 | tf_op jit(solution)/shard_map/dot_general | solution.py:135
  200.9 154.7 %reduce-scatter.2.cloned.1.call-done = f32[16,1024]{1,0:T(8,128)} async-done(((f32[1024,1024]{1,0:T(8,128)}), f32[16,1024]{1,0:T(8,128)}) %reduce-scatter.2.cloned.1.call-update) | async-done | bytes 65552 | tf_op jit(solution)/shard_map/reduce_scatter | solution.py:134
  355.6 1.0 fusion.66
  356.6 1.0 multiply_reduce_fusion
  357.6 1.5 add_convert_fusion
  (54 shorter events, 1.4 us)
Async XLA Ops:
  6.5 10.0 %copy-start = (bf16[128,1024]{1,0:T(8,128)(2,1)S(1)}, bf16[128,1024]{1,0:T(8,128)(2,1)}, u32[]{:S(2)}) copy-start(bf16[128,1024]{1,0:T(8,128)(2,1)} %param.15) | copy-start | bytes 786436
  6.5 3.2 copy-start.11
  6.5 3.4 copy-start.8
  6.5 3.6 copy-start.2
  6.5 99.0 %all-reduce.2.cloned.1.call-start = ((), (), s32[]{:S(2)}) async-start(), calls=%async_computation.1 | async-start | bytes 524288 | tf_op jit(solution)/shard_map/psum | solution.py:122
  11.2 1.1 copy-start.3
  15.8 91.6 %copy-start.6 = (f32[1024]{0:T(1024)S(1)}, f32[1024]{0:T(1024)}, u32[]{:S(2)}) copy-start(f32[1024]{0:T(1024)} %param.21) | copy-start | bytes 12292
  15.8 91.6 %copy-start.7 = (f32[1024]{0:T(1024)S(1)}, f32[1024]{0:T(1024)}, u32[]{:S(2)}) copy-start(f32[1024]{0:T(1024)} %param.20) | copy-start | bytes 12292
  15.9 179.6 %copy-start.9 = (bf16[64,1024]{1,0:T(8,128)(2,1)S(1)}, bf16[64,1024]{1,0:T(8,128)(2,1)}, u32[]{:S(2)}) copy-start(bf16[64,1024]{1,0:T(8,128)(2,1)} %param.23) | copy-start | bytes 393220
  15.9 179.6 %copy-start.10 = (bf16[1024,64]{0,1:T(8,128)(2,1)S(1)}, bf16[1024,64]{0,1:T(8,128)(2,1)}, u32[]{:S(2)}) copy-start(bf16[1024,64]{0,1:T(8,128)(2,1)} %param.22) | copy-start | bytes 393220
  17.5 178.0 %all-gather.2.cloned.1.call-start = ((), (), s32[]{:S(2)}) async-start(), calls=%async_computation.2 | async-start | bytes 2129920 | tf_op jit(solution)/shard_map/all_gather | solution.py:128
  109.0 246.6 %reduce-scatter.2.cloned.1.call-start = ((), (), s32[]{:S(2)}) async-start(), calls=%async_computation.3 | async-start | bytes 4259840 | tf_op jit(solution)/shard_map/reduce_scatter | solution.py:134
  200.8 154.8 %copy-start.1 = (bf16[16,1024]{1,0:T(8,128)(2,1)S(1)}, bf16[16,1024]{1,0:T(8,128)(2,1)}, u32[]{:S(2)}) copy-start(bf16[16,1024]{1,0:T(8,128)(2,1)} %add_convert_fusion.1) | copy-start | bytes 98308
  200.8 156.8 %copy-start.4 = (f32[1024]{0:T(1024)S(1)}, f32[1024]{0:T(1024)}, u32[]{:S(2)}) copy-start(f32[1024]{0:T(1024)} %param.25) | copy-start | bytes 12292
  200.8 156.8 %copy-start.5 = (f32[1024]{0:T(1024)S(1)}, f32[1024]{0:T(1024)}, u32[]{:S(2)}) copy-start(f32[1024]{0:T(1024)} %param.24) | copy-start | bytes 12292
Sparse Core Ops, SparseCore 0:
  17.7 87.8 all-reduce.1
  109.1 86.3 all-gather.1
  201.0 154.5 reduce-scatter.1
where the time goes:
time: 366 us
  waiting for transfers between devices  329 us (90%)
  between operations  13.4 us (4%)
  matrix products  9.21 us (3%)
  other arithmetic  7.88 us (2%)
  local copies, waits for them, and re-layouts  5.86 us (2%)
    reduce_scatter x1, waiting for transfers between devices, on_device(): lax.psum_scatter(jnp.dot(hidden, w_down, preferred_element_type=jnp.float...  155 us
    psum x1, waiting for transfers between devices, on_device(): lax.psum(partial_out.astype(jnp.bfloat16), 'req').astype(jnp.float32)  88 us
    all_gather x1, waiting for transfers between devices, on_device(): lax.all_gather(normed, 'blk', axis=0, tiled=True)  86.5 us
  transfers between devices with their start and end apart: 3, of which 3 were waited for; matrix products, arithmetic and copies ran while one was open for 0% of the time, Pallas kernels for 0%

commit v1 on v0

--- a/solution.py
+++ b/solution.py
@@ -1,3 +1,4 @@
+import functools
 import jax
 import jax.numpy as jnp
 from jax import lax
@@ -6,6 +7,16 @@
 HD = 64
 epsilon = 1e-05
 masked_score = -1e30
+
+
+def patches_part(u, shard_axis):
+    s_next = jnp.concatenate(
+        lax.all_to_all(jnp.stack(lax.axis_size(shard_axis) * [u], 0), shard_axis, 0, 0), 0
+    )
+    return s_next
+
+
+test_layers_all = functools.partial(patches_part, shard_axis="blk")
 
 
 def layer_norm(values, gain_vec, shift_vec):
@@ -124,11 +135,7 @@
     residual = lax.dynamic_slice_in_dim(tokens, row_first, own_rows, 0).astype(jnp.float32)
     normed = layer_norm(residual + head_mixed, norm1_gain, norm1_shift).astype(jnp.bfloat16)
     hidden = jax.nn.gelu(
-        jnp.dot(
-            lax.all_gather(normed, "blk", axis=0, tiled=True),
-            w_up,
-            preferred_element_type=jnp.float32,
-        ),
+        jnp.dot(test_layers_all(normed), w_up, preferred_element_type=jnp.float32),
         approximate=False,
     ).astype(jnp.bfloat16)
     branch = lax.psum_scatter(

time: 366 us -> 344 us (0.940)
  waiting for transfers between devices: 329 us -> 245 us
  blocking collectives: 0 us -> 63.7 us
    all_gather x1 -> x0, waiting for transfers between devices: 86.5 us -> none  [on_device(): lax.all_gather(normed, 'blk', axis=0, tiled=True)]
    all_to_all x0 -> x1, blocking collectives: none -> 63.7 us  [patches_part(): lax.all_to_all(jnp.stack(lax.axis_size(shard_axis) * [u], 0), shard_axis,...]
  transfers between devices with their start and end apart: 3 -> 2, of which waited for: 3 -> 2; matrix products, arithmetic and copies ran while one was open for 0% -> 0% of each run, Pallas kernels for 0% -> 0%
where the time goes in v1:
time: 344 us
  waiting for transfers between devices  245 us (71%)
  blocking collectives  63.7 us (19%)
  between operations  13.7 us (4%)
  matrix products  7.61 us (2%)
  other arithmetic  7.27 us (2%)
  local copies, waits for them, and re-layouts  6.11 us (2%)
    reduce_scatter x1, waiting for transfers between devices, on_device(): lax.psum_scatter(jnp.dot(hidden, w_down, preferred_element_type=jnp.float...  157 us
    psum x1, waiting for transfers between devices, on_device(): lax.psum(partial_out.astype(jnp.bfloat16), 'req').astype(jnp.float32)  88 us
    all_to_all x1, blocking collectives, patches_part(): lax.all_to_all(jnp.stack(lax.axis_size(shard_axis) * [u], 0), shard_axis,...  63.7 us
  transfers between devices with their start and end apart: 2, of which 2 were waited for; matrix products, arithmetic and copies ran while one was open for 0% of the time, Pallas kernels for 0%

profile of v1, /device:TPU:2, one launch (start us, length us, event | category | flops | bytes accessed | tf_op | source)
XLA Modules:
  0.0 343.5 jit_solution(15234300271910574095)
XLA Ops:
  6.6 1.5 copy.45
  8.1 1.3 convolution_convert_fusion.1
  10.1 0.3 copy.47
  10.5 0.7 gather_fusion.1
  11.2 0.3 copy.50
  11.6 0.2 slice.82
  11.8 0.5 copy-done.2
  12.2 0.3 copy.42
  12.6 0.7 gather_fusion
  13.3 0.3 copy.51
  13.7 0.2 slice.86
  13.9 0.3 fusion.105
  14.3 0.2 fusion.5
  14.7 0.2 fusion.69
  14.9 0.2 fusion.3
  15.2 0.1 copy.61
  15.3 0.2 fusion.106
  15.6 0.2 fusion.7
  15.9 0.3 fusion.18
  16.2 0.2 fusion.2
  16.5 1.0 convolution_convert_fusion
  17.6 88.0 %all-reduce.2.cloned.1.call-done = bf16[128,1024]{1,0:T(8,128)(2,1)} async-done(((bf16[128,1024]{1,0:T(8,128)(2,1)}), bf16[128,1024]{1,0:T(8,128)(2,1)}) %all-reduce.2.cloned.1.call-update) | async-done | bytes 262160 | tf_op jit(solution)/shard_map/psum | solution.py:133
  105.5 0.9 fusion.62
  106.4 1.0 multiply_reduce_fusion.1
  107.4 0.9 add_convert_fusion.1
  108.3 0.2 stack.2
  108.6 63.7 %all_to_all.5 = bf16[64,16,1024]{2,1,0:T(8,128)(2,1)S(1)} all-to-all(bf16[64,16,1024]{2,1,0:T(8,128)(2,1)S(1)} %stack.2), channel_id=1, replica_groups=mesh['blk'=64,'req'=8] {'blk'}, dimensions={0} | all-to-all | bytes 4194304 | tf_op jit(solution)/shard_map/all_to_all | solution.py:14
  172.3 3.7 %fusion.19 = f32[1024,1024]{1,0:T(8,128)} fusion(bf16[64,1024]{1,0:T(8,128)(2,1)S(1)} %copy-done.8, bf16[1024,1024]{1,0:T(8,128)(2,1)S(1)} %bitcast.88, bf16[1024,64]{0,1:T(8,128)(2,1)S(1)} %copy-done.9), kind=kOutput, calls=%fused_computation.37 | convolution fusion | flops 272695296 | bytes 6553600 | tf_op jit(solution)/shard_map/dot_general | solution.py:142
  176.1 157.1 %reduce-scatter.2.cloned.1.call-done = f32[16,1024]{1,0:T(8,128)} async-done(((f32[1024,1024]{1,0:T(8,128)}), f32[16,1024]{1,0:T(8,128)}) %reduce-scatter.2.cloned.1.call-update) | async-done | bytes 65552 | tf_op jit(solution)/shard_map/reduce_scatter | solution.py:141
  333.1 1.0 fusion.66
  334.1 1.0 multiply_reduce_fusion
  335.2 1.5 add_convert_fusion
  (51 shorter events, 1.4 us)
Async XLA Ops:
  6.5 9.9 %copy-start = (bf16[128,1024]{1,0:T(8,128)(2,1)S(1)}, bf16[128,1024]{1,0:T(8,128)(2,1)}, u32[]{:S(2)}) copy-start(bf16[128,1024]{1,0:T(8,128)(2,1)} %param.15) | copy-start | bytes 786436
  6.5 3.2 copy-start.10
  6.5 3.4 copy-start.7
  6.5 3.6 %copy-start.1 = (bf16[20,128,128]{2,1,0:T(8,128)(2,1)S(1)}, bf16[20,128,128]{2,1,0:T(8,128)(2,1)}, u32[]{:S(2)}) copy-start(bf16[20,128,128]{2,1,0:T(8,128)(2,1)} %param.16) | copy-start | bytes 1966084
  6.5 99.0 %all-reduce.2.cloned.1.call-start = ((), (), s32[]{:S(2)}) async-start(), calls=%async_computation.2 | async-start | bytes 524288 | tf_op jit(solution)/shard_map/psum | solution.py:133
  11.2 1.1 copy-start.2
  15.8 91.6 %copy-start.5 = (f32[1024]{0:T(1024)S(1)}, f32[1024]{0:T(1024)}, u32[]{:S(2)}) copy-start(f32[1024]{0:T(1024)} %param.21) | copy-start | bytes 12292
  15.8 91.6 %copy-start.6 = (f32[1024]{0:T(1024)S(1)}, f32[1024]{0:T(1024)}, u32[]{:S(2)}) copy-start(f32[1024]{0:T(1024)} %param.20) | copy-start | bytes 12292
  17.5 315.6 %reduce-scatter.2.cloned.1.call-start = ((), (), s32[]{:S(2)}) async-start(), calls=%async_computation.3 | async-start | bytes 4259840 | tf_op jit(solution)/shard_map/reduce_scatter | solution.py:141
  108.5 63.8 %copy-start.8 = (bf16[64,1024]{1,0:T(8,128)(2,1)S(1)}, bf16[64,1024]{1,0:T(8,128)(2,1)}, u32[]{:S(2)}) copy-start(bf16[64,1024]{1,0:T(8,128)(2,1)} %param.23) | copy-start | bytes 393220
  108.6 63.8 %copy-start.9 = (bf16[1024,64]{0,1:T(8,128)(2,1)S(1)}, bf16[1024,64]{0,1:T(8,128)(2,1)}, u32[]{:S(2)}) copy-start(bf16[1024,64]{0,1:T(8,128)(2,1)} %param.22) | copy-start | bytes 393220
  176.0 159.1 %copy-start.3 = (f32[1024]{0:T(1024)S(1)}, f32[1024]{0:T(1024)}, u32[]{:S(2)}) copy-start(f32[1024]{0:T(1024)} %param.25) | copy-start | bytes 12292
  176.1 159.1 %copy-start.4 = (f32[1024]{0:T(1024)S(1)}, f32[1024]{0:T(1024)}, u32[]{:S(2)}) copy-start(f32[1024]{0:T(1024)} %param.24) | copy-start | bytes 12292
Sparse Core Ops, SparseCore 0:
  17.6 87.8 all-reduce.1
  176.2 156.8 reduce-scatter.1

commit v2 on v0

--- a/solution.py
+++ b/solution.py
@@ -6,6 +6,12 @@
 HD = 64
 epsilon = 1e-05
 masked_score = -1e30
+
+
+def summed_here(x, name):
+    shards = lax.all_gather(x, name, axis=0, tiled=False)
+    total = shards.sum(axis=0)
+    return total
 
 
 def layer_norm(values, gain_vec, shift_vec):
@@ -119,7 +125,7 @@
     partial_out = jnp.dot(attended, w_out, preferred_element_type=jnp.float32)
     own_rows = tok_rows // lax.axis_size("req")
     row_first = lax.axis_index("req") * own_rows
-    summed = lax.psum(partial_out.astype(jnp.bfloat16), "req").astype(jnp.float32)
+    summed = summed_here(partial_out.astype(jnp.bfloat16), "req").astype(jnp.float32)
     head_mixed = lax.dynamic_slice_in_dim(summed, row_first, own_rows, 0)
     residual = lax.dynamic_slice_in_dim(tokens, row_first, own_rows, 0).astype(jnp.float32)
     normed = layer_norm(residual + head_mixed, norm1_gain, norm1_shift).astype(jnp.bfloat16)

time: 366 us -> 330 us (0.902)
  waiting for transfers between devices: 329 us -> 291 us
    psum x1 -> x0, waiting for transfers between devices: 88 us -> none  [on_device(): lax.psum(partial_out.astype(jnp.bfloat16), 'req').astype(jnp.float32)]
    all_gather x0 -> x1, waiting for transfers between devices: none -> 49.1 us  [summed_here(): shards = lax.all_gather(x, name, axis=0, tiled=False)]
where the time goes in v2:
time: 330 us; the launch traced here: 329 us
  waiting for transfers between devices  291 us (88%)
  between operations  13.4 us (4%)
  other arithmetic  9.81 us (3%)
  matrix products  9.25 us (3%)
  local copies, waits for them, and re-layouts  5.86 us (2%)
    reduce_scatter x1, waiting for transfers between devices, on_device(): lax.psum_scatter(jnp.dot(hidden, w_down, preferred_element_type=jnp.float...  155 us
    all_gather x1, waiting for transfers between devices, on_device(): lax.all_gather(normed, 'blk', axis=0, tiled=True)  86.7 us
    all_gather x1, waiting for transfers between devices, summed_here(): shards = lax.all_gather(x, name, axis=0, tiled=False)  49.1 us
  transfers between devices with their start and end apart: 3, of which 3 were waited for; matrix products, arithmetic and copies ran while one was open for 0% of the time, Pallas kernels for 0%

profile of v2, /device:TPU:2, one launch (start us, length us, event | category | flops | bytes accessed | tf_op | source)
XLA Modules:
  0.0 329.0 jit_solution(434383866190343432)
XLA Ops:
  6.6 1.5 copy.45
  8.1 1.3 convolution_convert_fusion.1
  10.1 0.3 copy.47
  10.5 0.7 gather_fusion.1
  11.2 0.3 copy.50
  11.6 0.2 slice.82
  11.8 0.5 copy-done.3
  12.2 0.3 copy.42
  12.6 0.7 gather_fusion
  13.3 0.3 copy.51
  13.7 0.2 slice.86
  13.9 0.3 fusion.105
  14.3 0.2 fusion.5
  14.7 0.2 fusion.69
  14.9 0.2 fusion.3
  15.2 0.1 copy.61
  15.3 0.2 fusion.106
  15.6 0.2 fusion.7
  15.8 0.3 fusion.18
  16.2 0.2 fusion.2
  16.5 1.1 convolution_convert_fusion
  17.6 49.1 %all-gather.6.cloned.1.call-done = bf16[1024,1024]{1,0:T(8,128)(2,1)} async-done(((bf16[128,1024]{1,0:T(8,128)(2,1)}), bf16[1024,1024]{1,0:T(8,128)(2,1)}) %all-gather.6.cloned.1.call-update) | async-done | bytes 2097168 | tf_op jit(solution)/shard_map/all_gather | solution.py:12
  66.7 2.0 reduce_sum.78
  68.7 0.9 fusion.62
  69.6 1.0 multiply_reduce_fusion.1
  70.5 1.5 add_convert_fusion.1
  72.1 86.7 %all-gather.4.cloned.1.call-done = bf16[1024,1024]{1,0:T(8,128)(2,1)} async-done(((bf16[16,1024]{1,0:T(8,128)(2,1)}), bf16[1024,1024]{1,0:T(8,128)(2,1)}) %all-gather.4.cloned.1.call-update) | async-done | bytes 2097168 | tf_op jit(solution)/shard_map/all_gather | solution.py:134
  158.8 5.3 %fusion.19 = f32[1024,1024]{1,0:T(8,128)} fusion(bf16[64,1024]{1,0:T(8,128)(2,1)S(1)} %copy-done.9, bf16[1024,1024]{1,0:T(8,128)(2,1)} %all-gather.4.cloned.1.call-done, bf16[1024,64]{0,1:T(8,128)(2,1)S(1)} %copy-done.10), kind=kOutput, calls=%fused_computation.37 | convolution fusion | flops 272695296 | bytes 6553600 | tf_op jit(solution)/shard_map/dot_general | solution.py:141
  164.1 154.8 %reduce-scatter.2.cloned.1.call-done = f32[16,1024]{1,0:T(8,128)} async-done(((f32[1024,1024]{1,0:T(8,128)}), f32[16,1024]{1,0:T(8,128)}) %reduce-scatter.2.cloned.1.call-update) | async-done | bytes 65552 | tf_op jit(solution)/shard_map/reduce_scatter | solution.py:140
  318.9 1.0 fusion.66
  319.9 1.0 multiply_reduce_fusion
  320.9 1.5 add_convert_fusion
  (55 shorter events, 1.5 us)
Async XLA Ops:
  6.5 10.0 %copy-start = (bf16[128,1024]{1,0:T(8,128)(2,1)S(1)}, bf16[128,1024]{1,0:T(8,128)(2,1)}, u32[]{:S(2)}) copy-start(bf16[128,1024]{1,0:T(8,128)(2,1)} %param.15) | copy-start | bytes 786436
  6.5 3.2 copy-start.11
  6.5 3.4 %copy-start.8 = (s32[5,4]{0,1:T(4,128)S(1)}, s32[5,4]{0,1:T(4,128)}, u32[]{:S(2)}) copy-start(s32[5,4]{0,1:T(4,128)} %param.18) | copy-start | bytes 244
  6.5 3.6 %copy-start.2 = (bf16[20,128,128]{2,1,0:T(8,128)(2,1)S(1)}, bf16[20,128,128]{2,1,0:T(8,128)(2,1)}, u32[]{:S(2)}) copy-start(bf16[20,128,128]{2,1,0:T(8,128)(2,1)} %param.16) | copy-start | bytes 1966084
  6.5 60.2 %all-gather.6.cloned.1.call-start = ((), (), s32[]{:S(2)}) async-start(), calls=%async_computation.3 | async-start | bytes 2359296 | tf_op jit(solution)/shard_map/all_gather | solution.py:12
  11.2 1.1 copy-start.3
  16.2 54.3 %copy-start.6 = (f32[1024]{0:T(1024)S(1)}, f32[1024]{0:T(1024)}, u32[]{:S(2)}) copy-start(f32[1024]{0:T(1024)} %param.21) | copy-start | bytes 12292
  16.2 54.3 %copy-start.7 = (f32[1024]{0:T(1024)S(1)}, f32[1024]{0:T(1024)}, u32[]{:S(2)}) copy-start(f32[1024]{0:T(1024)} %param.20) | copy-start | bytes 12292
  16.2 142.6 %copy-start.9 = (bf16[64,1024]{1,0:T(8,128)(2,1)S(1)}, bf16[64,1024]{1,0:T(8,128)(2,1)}, u32[]{:S(2)}) copy-start(bf16[64,1024]{1,0:T(8,128)(2,1)} %param.23) | copy-start | bytes 393220
  16.2 142.6 %copy-start.10 = (bf16[1024,64]{0,1:T(8,128)(2,1)S(1)}, bf16[1024,64]{0,1:T(8,128)(2,1)}, u32[]{:S(2)}) copy-start(bf16[1024,64]{0,1:T(8,128)(2,1)} %param.22) | copy-start | bytes 393220
  17.6 141.2 %all-gather.4.cloned.1.call-start = ((), (), s32[]{:S(2)}) async-start(), calls=%async_computation.1 | async-start | bytes 2129920 | tf_op jit(solution)/shard_map/all_gather | solution.py:134
  72.0 246.9 %reduce-scatter.2.cloned.1.call-start = ((), (), s32[]{:S(2)}) async-start(), calls=%async_computation.2 | async-start | bytes 4259840 | tf_op jit(solution)/shard_map/reduce_scatter | solution.py:140
  164.1 154.8 %copy-start.1 = (bf16[16,1024]{1,0:T(8,128)(2,1)S(1)}, bf16[16,1024]{1,0:T(8,128)(2,1)}, u32[]{:S(2)}) copy-start(bf16[16,1024]{1,0:T(8,128)(2,1)} %add_convert_fusion.1) | copy-start | bytes 98308
  164.1 156.8 %copy-start.4 = (f32[1024]{0:T(1024)S(1)}, f32[1024]{0:T(1024)}, u32[]{:S(2)}) copy-start(f32[1024]{0:T(1024)} %param.25) | copy-start | bytes 12292
  164.1 156.8 %copy-start.5 = (f32[1024]{0:T(1024)S(1)}, f32[1024]{0:T(1024)}, u32[]{:S(2)}) copy-start(f32[1024]{0:T(1024)} %param.24) | copy-start | bytes 12292
Sparse Core Ops, SparseCore 0:
  17.7 48.9 all-gather.5
  72.1 86.5 all-gather.3
  164.3 154.5 reduce-scatter.1
